TPU v7x, 256 devices: a whole 4x4x8 slice. The times are simulated.
256 devices in a mesh: img: 64 (over x, z, core), grp: 4 (over y).
Axes of the slice: x: 4, y: 4, z: 8, core: 2. Of those that a mesh axis runs over, the one named last changes fastest.
Arguments:
- desc: bfloat16 [256, 1024, 256], P(('img', 'grp')), may hold values from -20 to 20
- w_proj: bfloat16 [256, 512], replicated, may hold values from -0.375 to 0.375
- w_out: bfloat16 [256, 256], replicated, may hold values from -0.375 to 0.375
- pair_list: int32 [1280, 2], P(('img', 'grp')), may hold values from 0 to 255, as said below
- pair_count: int32 [256], P(('img', 'grp')), may hold values from 1 to 5, as said below
Outputs:
- updated: bfloat16 [256, 1024, 256], P(('img', 'grp'))
Inputs may be any that keep to these rules, and one draw needn't show every extreme that they name: `pair_list`: for a slot of the device at img index i, the first image lies in column i (ids i * 4 to i * 4 + 3) and the second in column i or column (i + 1) % 64, and the two ids differ; every slot holds such a pair, live or not. `pair_count`: some device has all 5 slots live.
All inputs are finite; a program needn't handle non-finite values.
Results may differ from a plain program's by a relative error of at most 0.0072.
Values may be sent and summed in bfloat16 or wider, within the bound.
No kernel may reach another device: no remote copies, remote signals or barrier semaphores. Data moves between devices by JAX's collectives and lax.ppermute only.
A program may use at most 64 MiB of HBM per device.

v0:
```python
import jax
import jax.numpy as jnp
from jax import lax
from jax.sharding import PartitionSpec as P

D = 256
HEADS = 4
HEAD_DIM = 64


def from_behind(block, axis, distance):
    devices = range(lax.axis_size(axis))
    route = [((i - distance) % len(devices), i) for i in devices]
    return lax.ppermute(block, axis, route)


def pair_messages(first_rows, second_rows):
    to_first = []
    to_second = []
    for head_index in range(HEADS):
        lower = head_index * HEAD_DIM
        query_first = first_rows[:, lower : lower + HEAD_DIM]
        query_second = second_rows[:, lower : lower + HEAD_DIM]
        value_first = first_rows[:, D + lower : D + lower + HEAD_DIM]
        value_second = second_rows[:, D + lower : D + lower + HEAD_DIM]
        scores = jnp.dot(
            query_first, query_second.T, preferred_element_type=jnp.float32
        ) * HEAD_DIM ** (-0.5)
        across = jnp.exp(scores - jnp.max(scores, axis=1, keepdims=True))
        across = (across / jnp.sum(across, axis=1, keepdims=True)).astype(jnp.bfloat16)
        downward = jnp.exp(scores - jnp.max(scores, axis=0, keepdims=True))
        downward = (downward / jnp.sum(downward, axis=0, keepdims=True)).astype(jnp.bfloat16)
        to_first.append(jnp.dot(across, value_second, preferred_element_type=jnp.float32))
        to_second.append(
            lax.dot_general(
                downward, value_first, (((0,), (0,)), ((), ())), preferred_element_type=jnp.float32
            )
        )
    return (
        jnp.concatenate(to_first, 1).astype(jnp.bfloat16),
        jnp.concatenate(to_second, 1).astype(jnp.bfloat16),
    )


def window_slot(image_ids, column_index, columns, members):
    return (image_ids // members - column_index) % columns * members + image_ids % members


def on_device(desc, w_proj, w_out, pair_list, pair_count):
    columns = lax.axis_size("img")
    members = lax.axis_size("grp")
    column_index = lax.axis_index("img")
    keypoints = desc.shape[1]
    own_rows = jnp.dot(desc[0], w_proj, preferred_element_type=jnp.float32).astype(jnp.bfloat16)[
        None
    ]
    group_rows = lax.all_gather(own_rows, "grp", axis=0, tiled=True)
    next_rows = from_behind(group_rows, "img", -1)
    window = jnp.concatenate([group_rows, next_rows], 0)
    live_count = pair_count[0]
    slots = window_slot(pair_list, column_index, columns, members)

    def visit(position, totals):
        first_slot = slots[position, 0]
        second_slot = slots[position, 1]
        first_rows = lax.dynamic_index_in_dim(window, first_slot, 0, keepdims=False)
        second_rows = lax.dynamic_index_in_dim(window, second_slot, 0, keepdims=False)
        to_first, to_second = pair_messages(first_rows, second_rows)
        totals = totals.at[first_slot].add(to_first.astype(jnp.float32))
        return totals.at[second_slot].add(to_second.astype(jnp.float32))

    totals = jnp.zeros((2 * members, keypoints, D), jnp.float32)
    totals = lax.fori_loop(0, live_count, visit, totals)
    returned = from_behind(totals[members:], "img", 1)
    summed = lax.psum_scatter(totals[:members] + returned, "grp", scatter_dimension=0, tiled=True)
    message = summed[0].astype(jnp.bfloat16)
    update = jnp.dot(message, w_out, preferred_element_type=jnp.float32)
    return (desc[0].astype(jnp.float32) + update).astype(jnp.bfloat16)[None]


def solution(mesh):
    return jax.shard_map(
        on_device,
        mesh=mesh,
        in_specs=(
            P(("img", "grp"), None, None),
            P(),
            P(),
            P(("img", "grp"), None),
            P(("img", "grp")),
        ),
        out_specs=P(("img", "grp"), None, None),
        check_vma=False,
    )
```

profile of v0, /device:TPU:1, one launch (start us, length us, event | category | flops | bytes accessed | tf_op | source)
XLA Modules:
  0.0 399.2 jit_solution(12478828602547499768)
XLA Ops:
  7.5 2.5 convolution_convert_fusion
  10.0 54.8 %all-gather.3.cloned.1.call-done = bf16[4096,512]{1,0:T(8,128)(2,1)} async-done(((bf16[1024,512]{1,0:T(8,128)(2,1)}), bf16[4096,512]{1,0:T(8,128)(2,1)}) %all-gather.3.cloned.1.call-update) | async-done | bytes 4194320 | tf_op jit(solution)/shard_map/all_gather | solution.py:57
  66.2 47.0 %collective-permute-done = bf16[4,1024,512]{2,1,0:T(8,128)(2,1)} collective-permute-done((bf16[4,1024,512]{2,1,0:T(8,128)(2,1)}, bf16[4,1024,512]{2,1,0:T(8,128)(2,1)}, u32[]{:S(2)}, u32[]{:S(2)}) %collective-permute-start) | collective-permute-done | bytes 4194336 | tf_op jit(solution)/shard_map/ppermute | solution.py:14
  113.1 7.4 %pad_maximum_fusion = bf16[8,1024,512]{2,1,0:T(8,128)(2,1)} fusion(bf16[4,1024,512]{2,1,0:T(8,128)(2,1)} %collective-permute-done, bf16[4,1024,512]{2,1,0:T(8,128)(2,1)} %bitcast.64), kind=kLoop, calls=%fused_computation.98 | loop fusion | flops 4194304 | bytes 16777216 | tf_op jit(solution)/shard_map/concatenate | solution.py:59
  120.5 4.3 %broadcast_in_dim.6 = f32[8,1024,256]{1,2,0:T(8,128)} broadcast(f32[]{:T(128)} %constant.102.clone.1), dimensions={} | broadcast | bytes 8388612 | tf_op jit(solution)/shard_map/broadcast_in_dim | solution.py:72
  124.8 65.9 %while.12 = (s32[]{:T(128)}, f32[8,1024,256]{1,2,0:T(8,128)}, s32[]{:T(128)}, s32[5,2]{0,1:T(2,128)S(1)}, bf16[8,1024,512]{2,1,0:T(8,128)(2,1)}, /*index=5*/s32[...) while((s32[]{:T(128)}, f32[8,1024,256]{1,2,0:T(8,128)}, s32[]{:T(128)}, ...), condition=%wide.region_19.20_spmd, body=%wide.region_0.19_spmd.sunk | while | flops 1683472384 | bytes 81955088 | solution.py:73
  131.0 1.7 dynamic-slice_bitcast_fusion.3
  133.5 1.6 fusion.108
  135.0 1.3 fusion.109
  138.2 1.6 fusion.106
  139.7 1.2 fusion.107
  142.8 1.6 fusion.104
  144.3 1.2 fusion.105
  147.4 1.6 fusion.102
  150.0 1.2 fusion.103
  151.3 3.0 fusion.110
  154.3 3.1 fusion.115
  163.5 1.7 dynamic-slice_bitcast_fusion.3
  165.9 1.6 fusion.108
  167.5 1.3 fusion.109
  170.6 1.6 fusion.106
  172.2 1.2 fusion.107
  175.2 1.6 fusion.104
  179.9 1.6 fusion.102
  182.5 1.2 fusion.103
  183.7 3.0 fusion.110
  186.8 3.1 fusion.115
  190.8 2.7 slice.93
  193.5 45.4 %collective-permute-done.1 = f32[4,1024,256]{1,2,0:T(8,128)S(1)} collective-permute-done((f32[4,1024,256]{1,2,0:T(8,128)S(1)}, f32[4,1024,256]{1,2,0:T(8,128)S(1)}, u32[]{:S(2)}, u32[]{:S(2)}) %collective-permute-start.1) | collective-permute-done | bytes 4194336 | tf_op jit(solution)/shard_map/ppermute | solution.py:14
  239.0 2.9 slice_add_fusion
  241.8 148.2 %reduce-scatter.2.cloned.1.call-done = f32[1,1024,256]{1,2,0:T(8,128)} async-done(((f32[4,1024,256]{1,2,0:T(8,128)}), f32[1,1024,256]{1,2,0:T(8,128)}) %reduce-scatter.2.cloned.1.call-update) | async-done | bytes 1048592 | tf_op jit(solution)/shard_map/reduce_scatter | solution.py:75
  390.0 2.4 fusion.63
  (38 shorter events, 21.4 us)
Async XLA Ops:
  6.5 1.0 copy-start
  6.5 58.2 %all-gather.3.cloned.1.call-start = ((), (), s32[]{:S(2)}) async-start(), calls=%async_computation.2 | async-start | bytes 5242880 | tf_op jit(solution)/shard_map/all_gather | solution.py:57
  10.0 380.1 %reduce-scatter.2.cloned.1.call-start = ((), (), s32[]{:S(2)}) async-start(), calls=%async_computation.1 | async-start | bytes 5242880 | tf_op jit(solution)/shard_map/reduce_scatter | solution.py:75
  64.8 48.3 %collective-permute-start = (bf16[4,1024,512]{2,1,0:T(8,128)(2,1)}, bf16[4,1024,512]{2,1,0:T(8,128)(2,1)}, u32[]{:S(2)}, u32[]{:S(2)}) collective-permute-start(bf16[4,1024,512]{2,1,0:T(8,128)(2,1)} %bitcast.63), channel_id=1, source_target_pairs={{4,0},{8,4},{12,8},{16,12},{20,16},{24,20},{28,24},{32,28},{36,32}... | collective-permute-start | bytes 12582920 | tf_op jit(solution)/shard_map/ppermute | solution.py:14
  120.5 4.3 %copy-start.4 = (s32[3]{0:T(128)S(1)}, s32[3]{0:T(128)}, u32[]{:S(2)}) copy-start(s32[3]{0:T(128)} %constant.96.clone.1) | copy-start | bytes 40
  190.8 48.2 %copy-start.1 = (f32[8,1024,256]{1,2,0:T(8,128)S(1)}, f32[8,1024,256]{1,2,0:T(8,128)}, u32[]{:S(2)}) copy-start(f32[8,1024,256]{1,2,0:T(8,128)} %get-tuple-element.57) | copy-start | bytes 25165828
  193.4 45.5 %collective-permute-start.1 = (f32[4,1024,256]{1,2,0:T(8,128)S(1)}, f32[4,1024,256]{1,2,0:T(8,128)S(1)}, u32[]{:S(2)}, u32[]{:S(2)}) collective-permute-start(f32[4,1024,256]{1,2,0:T(8,128)S(1)} %slice.93), channel_id=1, source_target_pairs={{252,0},{0,4},{4,8},{8,12},{12,16},{16,20},{20,24},{24,28},{28,32}... | collective-permute-start | bytes 12582920 | tf_op jit(solution)/shard_map/ppermute | solution.py:14
  241.8 148.2 %copy-start.2 = (bf16[1,1024,256]{2,1,0:T(8,128)(2,1)S(1)}, bf16[1,1024,256]{2,1,0:T(8,128)(2,1)}, u32[]{:S(2)}) copy-start(bf16[1,1024,256]{2,1,0:T(8,128)(2,1)} %param.11) | copy-start | bytes 1572868
  241.8 148.2 %copy-start.3 = (bf16[256,256]{1,0:T(8,128)(2,1)S(1)}, bf16[256,256]{1,0:T(8,128)(2,1)}, u32[]{:S(2)}) copy-start(bf16[256,256]{1,0:T(8,128)(2,1)} %param.13) | copy-start | bytes 393220
Sparse Core Ops, SparseCore 0:
  10.1 54.6 all-gather.2
  242.0 148.0 reduce-scatter.1
where the time goes:
time: 400 us; the launch traced here: 399 us
  waiting for transfers between devices  295 us (74%)
  other arithmetic  37.2 us (9%)
  matrix products  29.6 us (7%)
  between operations  13.4 us (3%)
  local copies, waits for them, and re-layouts  12.6 us (3%)
  loops' own time  10.2 us (3%)
    reduce_scatter x1, waiting for transfers between devices, on_device(): lax.psum_scatter(totals[:members] + returned, 'grp', scatter_dimension=0,...  148 us
    ppermute x2, waiting for transfers between devices, from_behind(): return lax.ppermute(block, axis, route)  92.4 us
    all_gather x1, waiting for transfers between devices, on_device(): group_rows = lax.all_gather(own_rows, 'grp', axis=0, tiled=True)  54.8 us
    reduce_sum x8, other arithmetic, pair_messages(): jnp.sum(downward, axis=0, keepdims=True)  12.4 us
    another operation x1, loops' own time, on_device(): totals = lax.fori_loop(0, live_count, visit, totals)  10.2 us
    dot_general x8, matrix products, pair_messages(): jnp.dot(across, value_second, preferred_element_type=jnp.float32)  9.98 us
    dot_general x8, matrix products, pair_messages(): lax.dot_general(downward, value_first, (((0,), (0,)), ((), ())), preferre...  8.13 us
  transfers between devices with their start and end apart: 4, of which 4 were waited for; matrix products, arithmetic and copies ran while one was open for 0% of the time, Pallas kernels for 0%

commit v1 on v0

--- a/solution.py
+++ b/solution.py
@@ -2,6 +2,7 @@
 import jax.numpy as jnp
 from jax import lax
 from jax.sharding import PartitionSpec as P
+from jax.lax import axis_index, axis_size, ppermute
 
 D = 256
 HEADS = 4
@@ -54,7 +55,19 @@
     own_rows = jnp.dot(desc[0], w_proj, preferred_element_type=jnp.float32).astype(jnp.bfloat16)[
         None
     ]
-    group_rows = lax.all_gather(own_rows, "grp", axis=0, tiled=True)
+
+    def manage_set(point, axis_k):
+        shares = axis_size("grp")
+        res = [(ii - 1, ii) for ii in range(1, shares)] + [(shares - 1, 0)]
+        mat_out = point
+        so_far_all = [mat_out]
+        for _ in range(shares - 1):
+            mat_out = ppermute(mat_out, "grp", res)
+            so_far_all += [mat_out]
+        z_new = jnp.concatenate([*reversed(so_far_all)], axis_k)
+        return jnp.roll(z_new, (axis_index("grp") + 1) * mat_out.shape[axis_k], axis=axis_k)
+
+    group_rows = manage_set(own_rows, 0)
     next_rows = from_behind(group_rows, "img", -1)
     window = jnp.concatenate([group_rows, next_rows], 0)
     live_count = pair_count[0]

time: 400 us -> 428 us (1.070)
  waiting for transfers between devices: 295 us -> 310 us
  starting transfers between devices: 0.8 us -> 9.33 us
  local copies, waits for them, and re-layouts: 12.6 us -> 17.8 us
    ppermute x0 -> x3, waiting for transfers between devices: none -> 65.8 us  [manage_set(): mat_out = ppermute(mat_out, 'grp', res)]
    all_gather x1 -> x0, waiting for transfers between devices: 54.8 us -> none  [on_device(): group_rows = lax.all_gather(own_rows, 'grp', axis=0, tiled=True)]
    ppermute x0 -> x3, starting transfers between devices: none -> 4.64 us  [manage_set(): mat_out = ppermute(mat_out, 'grp', res)]
  transfers between devices with their start and end apart: 4 -> 6, of which waited for: 4 -> 6; matrix products, arithmetic and copies ran while one was open for 0% -> 0% of each run, Pallas kernels for 0% -> 0%
where the time goes in v1:
time: 428 us; the launch traced here: 426 us
  waiting for transfers between devices  310 us (72%)
  other arithmetic  36.6 us (9%)
  matrix products  28.6 us (7%)
  local copies, waits for them, and re-layouts  17.8 us (4%)
  between operations  13.5 us (3%)
  loops' own time  10.2 us (2%)
  starting transfers between devices  9.33 us (2%)
    reduce_scatter x1, waiting for transfers between devices, on_device(): lax.psum_scatter(totals[:members] + returned, 'grp', scatter_dimension=0,...  149 us
    ppermute x2, waiting for transfers between devices, from_behind(): return lax.ppermute(block, axis, route)  96 us
    ppermute x3, waiting for transfers between devices, manage_set(): mat_out = ppermute(mat_out, 'grp', res)  65.8 us
    reduce_sum x8, other arithmetic, pair_messages(): jnp.sum(downward, axis=0, keepdims=True)  12.4 us
    another operation x1, loops' own time, on_device(): totals = lax.fori_loop(0, live_count, visit, totals)  10.2 us
    dot_general x8, matrix products, pair_messages(): jnp.dot(across, value_second, preferred_element_type=jnp.float32)  9.98 us
  transfers between devices with their start and end apart: 6, of which 6 were waited for; matrix products, arithmetic and copies ran while one was open for 0% of the time, Pallas kernels for 0%

profile of v1, /device:TPU:1, one launch (start us, length us, event | category | flops | bytes accessed | tf_op | source)
XLA Modules:
  0.0 426.4 jit_solution(13537211583850164748)
XLA Ops:
  7.5 1.5 fusion.62
  9.0 2.2 collective-permute-start
  11.2 22.3 %collective-permute-done = bf16[1,1024,512]{2,1,0:T(8,128)(2,1)S(1)} collective-permute-done((bf16[1,1024,512]{2,1,0:T(8,128)(2,1)S(1)}, bf16[1,1024,512]{2,1,0:T(8,128)(2,1)S(1)}, u32[]{:S(2)}, u32[]{:S(2)}) %collective-permute-start) | collective-permute-done | bytes 1048608 | tf_op jit(solution)/shard_map/ppermute | solution.py:65
  33.5 1.6 collective-permute-start.1
  35.0 22.0 %collective-permute-done.1 = bf16[1,1024,512]{2,1,0:T(8,128)(2,1)S(1)} collective-permute-done((bf16[1,1024,512]{2,1,0:T(8,128)(2,1)S(1)}, bf16[1,1024,512]{2,1,0:T(8,128)(2,1)S(1)}, u32[]{:S(2)}, u32[]{:S(2)}) %collective-permute-start.1) | collective-permute-done | bytes 1048608 | tf_op jit(solution)/shard_map/ppermute | solution.py:65
  57.9 21.4 %collective-permute-done.2 = bf16[1,1024,512]{2,1,0:T(8,128)(2,1)} collective-permute-done((bf16[1,1024,512]{2,1,0:T(8,128)(2,1)S(1)}, bf16[1,1024,512]{2,1,0:T(8,128)(2,1)}, u32[]{:S(2)}, u32[]{:S(2)}) %collective-permute-start.2) | collective-permute-done | bytes 1048608 | tf_op jit(solution)/shard_map/ppermute | solution.py:65
  80.9 1.3 constant_dynamic-update-slice_fusion.3
  82.4 2.3 constant_dynamic-slice_fusion.2
  84.7 4.6 %collective-permute-start.3 = (bf16[4,1024,512]{2,1,0:T(8,128)(2,1)}, bf16[4,1024,512]{2,1,0:T(8,128)(2,1)}, u32[]{:S(2)}, u32[]{:S(2)}) collective-permute-start(bf16[4,1024,512]{2,1,0:T(8,128)(2,1)} %constant_dynamic-slice_fusion.2), channel_id=1, source_target_pairs={{4,0},{8,4},{12,8},{16,12},{20,16},{24,20},{28,24},{32,28},{36,32}... | collective-permute-start | bytes 12582920 | tf_op jit(solution)/shard_map/ppermute | solution.py:15
  89.3 50.5 %collective-permute-done.3 = bf16[4,1024,512]{2,1,0:T(8,128)(2,1)} collective-permute-done((bf16[4,1024,512]{2,1,0:T(8,128)(2,1)}, bf16[4,1024,512]{2,1,0:T(8,128)(2,1)}, u32[]{:S(2)}, u32[]{:S(2)}) %collective-permute-start.3) | collective-permute-done | bytes 4194336 | tf_op jit(solution)/shard_map/ppermute | solution.py:15
  139.8 7.4 %pad_maximum_fusion = bf16[8,1024,512]{2,1,0:T(8,128)(2,1)} fusion(bf16[4,1024,512]{2,1,0:T(8,128)(2,1)} %collective-permute-done.3, bf16[4,1024,512]{2,1,0:T(8,128)(2,1)} %constant_dynamic-slice_fusion.2), kind=kLoop, calls=%fused_computation.98 | loop fusion | flops 4194304 | bytes 16777216 | tf_op jit(solution)/shard_map/concatenate | solution.py:72
  147.3 4.3 %broadcast_in_dim.6 = f32[8,1024,256]{1,2,0:T(8,128)} broadcast(f32[]{:T(128)} %constant.120.clone.1), dimensions={} | broadcast | bytes 8388612 | tf_op jit(solution)/shard_map/broadcast_in_dim | solution.py:85
  151.5 65.9 %while.12 = (s32[]{:T(128)}, f32[8,1024,256]{1,2,0:T(8,128)}, s32[]{:T(128)}, s32[5,2]{0,1:T(2,128)S(1)}, bf16[8,1024,512]{2,1,0:T(8,128)(2,1)}, /*index=5*/s32[...) while((s32[]{:T(128)}, f32[8,1024,256]{1,2,0:T(8,128)}, s32[]{:T(128)}, ...), condition=%wide.region_19.20_spmd, body=%wide.region_0.19_spmd.sunk | while | flops 1683472384 | bytes 81955088 | solution.py:86
  157.7 1.7 dynamic-slice_bitcast_fusion.3
  160.2 1.6 fusion.109
  164.9 1.6 fusion.107
  169.5 1.6 fusion.105
  174.2 1.6 fusion.103
  178.0 3.0 fusion.111
  181.0 3.1 fusion.116
  190.2 1.7 dynamic-slice_bitcast_fusion.3
  192.6 1.6 fusion.109
  197.3 1.6 fusion.107
  201.9 1.6 fusion.105
  206.6 1.6 fusion.103
  210.5 3.0 fusion.111
  213.5 3.1 fusion.116
  217.5 2.7 slice.93
  220.2 45.4 %collective-permute-done.4 = f32[4,1024,256]{1,2,0:T(8,128)S(1)} collective-permute-done((f32[4,1024,256]{1,2,0:T(8,128)S(1)}, f32[4,1024,256]{1,2,0:T(8,128)S(1)}, u32[]{:S(2)}, u32[]{:S(2)}) %collective-permute-start.4) | collective-permute-done | bytes 4194336 | tf_op jit(solution)/shard_map/ppermute | solution.py:15
  265.7 2.9 slice_add_fusion
  268.6 148.6 %reduce-scatter.2.cloned.1.call-done = f32[1,1024,256]{1,2,0:T(8,128)} async-done(((f32[4,1024,256]{1,2,0:T(8,128)}), f32[1,1024,256]{1,2,0:T(8,128)}) %reduce-scatter.2.cloned.1.call-update) | async-done | bytes 1048592 | tf_op jit(solution)/shard_map/reduce_scatter | solution.py:88
  417.2 2.4 fusion.64
  (54 shorter events, 31.3 us)
Async XLA Ops:
  6.5 1.0 copy-start
  6.5 410.6 %reduce-scatter.2.cloned.1.call-start = ((), (), s32[]{:S(2)}) async-start(), calls=%async_computation.1 | async-start | bytes 5242880 | tf_op jit(solution)/shard_map/reduce_scatter | solution.py:88
  9.0 24.5 %collective-permute-start = (bf16[1,1024,512]{2,1,0:T(8,128)(2,1)S(1)}, bf16[1,1024,512]{2,1,0:T(8,128)(2,1)S(1)}, u32[]{:S(2)}, u32[]{:S(2)}) collective-permute-start(bf16[1,1024,512]{2,1,0:T(8,128)(2,1)S(1)} %fusion.62), channel_id=1, source_target_pairs={{0,1},{1,2},{2,3},{3,0},{4,5},{5,6},{6,7},{7,4},{8,9},{9,10},{10,1... | collective-permute-start | bytes 3145736 | tf_op jit(solution)/shard_map/ppermute | solution.py:65
  33.5 23.6 %collective-permute-start.1 = (bf16[1,1024,512]{2,1,0:T(8,128)(2,1)S(1)}, bf16[1,1024,512]{2,1,0:T(8,128)(2,1)S(1)}, u32[]{:S(2)}, u32[]{:S(2)}) collective-permute-start(bf16[1,1024,512]{2,1,0:T(8,128)(2,1)S(1)} %collective-permute-done), channel_id=1, source_target_pairs={{0,1},{1,2},{2,3},{3,0},{4,5},{5,6},{6,7},{7,4},{8,9},{9,10},{10,1... | collective-permute-start | bytes 3145736 | tf_op jit(solution)/shard_map/ppermute | solution.py:65
  57.1 22.3 %collective-permute-start.2 = (bf16[1,1024,512]{2,1,0:T(8,128)(2,1)S(1)}, bf16[1,1024,512]{2,1,0:T(8,128)(2,1)}, u32[]{:S(2)}, u32[]{:S(2)}) collective-permute-start(bf16[1,1024,512]{2,1,0:T(8,128)(2,1)S(1)} %collective-permute-done.1), channel_id=1, source_target_pairs={{0,1},{1,2},{2,3},{3,0},{4,5},{5,6},{6,7},{7,4},{8,9},{9,10},{10,1... | collective-permute-start | bytes 3145736 | tf_op jit(solution)/shard_map/ppermute | solution.py:65
  82.4 6.9 %copy-start.6 = (s32[5,2]{0,1:T(2,128)S(1)}, s32[5,2]{0,1:T(2,128)}, u32[]{:S(2)}) copy-start(s32[5,2]{0,1:T(2,128)} %param.14) | copy-start | bytes 124
  84.7 55.2 %collective-permute-start.3 = (bf16[4,1024,512]{2,1,0:T(8,128)(2,1)}, bf16[4,1024,512]{2,1,0:T(8,128)(2,1)}, u32[]{:S(2)}, u32[]{:S(2)}) collective-permute-start(bf16[4,1024,512]{2,1,0:T(8,128)(2,1)} %constant_dynamic-slice_fusion.2), channel_id=1, source_target_pairs={{4,0},{8,4},{12,8},{16,12},{20,16},{24,20},{28,24},{32,28},{36,32}... | collective-permute-start | bytes 12582920 | tf_op jit(solution)/shard_map/ppermute | solution.py:15
  147.3 4.3 %copy-start.5 = (s32[3]{0:T(128)S(1)}, s32[3]{0:T(128)}, u32[]{:S(2)}) copy-start(s32[3]{0:T(128)} %constant.114.clone.1) | copy-start | bytes 40
  217.5 48.2 %copy-start.2 = (f32[8,1024,256]{1,2,0:T(8,128)S(1)}, f32[8,1024,256]{1,2,0:T(8,128)}, u32[]{:S(2)}) copy-start(f32[8,1024,256]{1,2,0:T(8,128)} %get-tuple-element.57) | copy-start | bytes 25165828
  220.1 45.5 %collective-permute-start.4 = (f32[4,1024,256]{1,2,0:T(8,128)S(1)}, f32[4,1024,256]{1,2,0:T(8,128)S(1)}, u32[]{:S(2)}, u32[]{:S(2)}) collective-permute-start(f32[4,1024,256]{1,2,0:T(8,128)S(1)} %slice.93), channel_id=1, source_target_pairs={{252,0},{0,4},{4,8},{8,12},{12,16},{16,20},{20,24},{24,28},{28,32}... | collective-permute-start | bytes 12582920 | tf_op jit(solution)/shard_map/ppermute | solution.py:15
  265.7 153.9 %copy-start.1 = (bf16[256,512]{1,0:T(8,128)(2,1)S(1)}, bf16[256,512]{1,0:T(8,128)(2,1)}, u32[]{:S(2)}) copy-start(bf16[256,512]{1,0:T(8,128)(2,1)} %param.12) | copy-start | bytes 786436
  268.5 148.7 %copy-start.3 = (bf16[1,1024,256]{2,1,0:T(8,128)(2,1)S(1)}, bf16[1,1024,256]{2,1,0:T(8,128)(2,1)}, u32[]{:S(2)}) copy-start(bf16[1,1024,256]{2,1,0:T(8,128)(2,1)} %param.11) | copy-start | bytes 1572868
  268.5 148.7 %copy-start.4 = (bf16[256,256]{1,0:T(8,128)(2,1)S(1)}, bf16[256,256]{1,0:T(8,128)(2,1)}, u32[]{:S(2)}) copy-start(bf16[256,256]{1,0:T(8,128)(2,1)} %param.13) | copy-start | bytes 393220
Sparse Core Ops, SparseCore 0:
  268.7 148.4 reduce-scatter.1
